TPU v7x, 32 devices: a whole 2x2x4 slice. The times are simulated.
32 devices in a mesh: rows: 8 (over z, y), band: 4 (over x, core).
Axes of the slice: x: 2, y: 2, z: 4, core: 2. Of those that a mesh axis runs over, the one named last changes fastest.
Arguments:
- embedding: bfloat16 [1024, 512], P('rows'), may hold values from -6 to 6
- w_left: bfloat16 [512, 32], replicated, may hold values from -0.25 to 0.25
- w_right: bfloat16 [512, 32], replicated, may hold values from -0.25 to 0.25
- w_in: bfloat16 [32, 128], replicated, may hold values from -1 to 1
- w_out: bfloat16 [128, 32], replicated, may hold values from -0.5 to 0.5
- w_head: float32 [32], replicated, may hold values from -1 to 1
- dist_bias: float32 [32, 4], replicated, may hold values from -3 to 3
- offsets: int32 [8, 4], P('rows', 'band'), may hold values from 0 to 3, each once within a row
- valid_bins: int32 [1024], P('rows'), may hold values 0 or 1
- target: bfloat16 [8, 4, 128, 128], P('rows', 'band'), may hold values from -6 to 6
Outputs:
- predicted: bfloat16 [8, 4, 128, 128], P('rows', 'band')
- grad_embedding: bfloat16 [1024, 512], P('rows', 'band')
- grad_left: float32 [512, 32], replicated
- grad_right: float32 [512, 32], replicated
- grad_in: float32 [32, 128], replicated
- grad_out: float32 [128, 32], replicated
- grad_head: float32 [32], replicated
- grad_bias: float32 [32, 4], replicated
Inputs may be any that keep to these rules, and one draw needn't show every extreme that they name: `offsets`: each row tile's 4 entries are the numbers 0 to 3 in some order.
All inputs are finite; a program needn't handle non-finite values. No bound on the sum of `valid_bins` on one device may be relied on, other than what follows from the above.
Results may differ from a plain program's by a relative error of at most 0.0058.
Values may be sent and summed in bfloat16 or wider, within the bound.
No kernel may reach another device: no remote copies, remote signals or barrier semaphores. Data moves between devices by JAX's collectives and lax.ppermute only.
A program may use at most 64 MiB of HBM per device.

v0:
```python
import jax
import jax.numpy as jnp
from jax import lax
from jax.sharding import PartitionSpec as P

TILE = 128
NOFF = 4


def from_behind(value, axis, steps):
    count = lax.axis_size(axis)
    leading, last = (max(0, -steps), min(count, count - steps))
    return lax.ppermute(value, axis, [(source, source + steps) for source in range(leading, last)])


def gelu_pair(pre_act):
    return jax.nn.gelu(pre_act, approximate=True)


def block_terms(row_proj, col_proj, bias_col, row_flags, col_flags, goal_rows, w_in, w_out, w_head):
    channels = row_proj.shape[0]
    row_count = row_proj.shape[1]
    col_count = col_proj.shape[1]
    summed = (
        row_proj.astype(jnp.float32)[:, :, None]
        + col_proj.astype(jnp.float32)[:, None, :]
        + bias_col[:, None, None]
    )
    summed = summed.reshape(channels, row_count * col_count)
    pair_in = summed.astype(jnp.bfloat16)
    pre_act = lax.dot_general(
        w_in, pair_in, (((0,), (0,)), ((), ())), preferred_element_type=jnp.float32
    )
    activation = gelu_pair(pre_act).astype(jnp.bfloat16)
    update = summed + lax.dot_general(
        w_out, activation, (((0,), (0,)), ((), ())), preferred_element_type=jnp.float32
    )
    logits = jnp.dot(w_head, update, precision=lax.Precision.HIGHEST)
    weight_mask = (row_flags[:, None] * col_flags[None, :]).reshape(-1)
    residual = weight_mask * (logits - goal_rows.astype(jnp.float32).reshape(-1)) / (NOFF * TILE)
    grad_update = w_head[:, None] * residual[None, :]
    grad_low = grad_update.astype(jnp.bfloat16)
    head_term = jnp.dot(update, residual, precision=lax.Precision.HIGHEST)
    out_term = lax.dot_general(
        activation, grad_low, (((1,), (1,)), ((), ())), preferred_element_type=jnp.float32
    )
    grad_act = lax.dot_general(
        w_out, grad_low, (((1,), (0,)), ((), ())), preferred_element_type=jnp.float32
    )
    _, backward = jax.vjp(gelu_pair, pre_act)
    grad_pre = backward(grad_act)[0].astype(jnp.bfloat16)
    in_term = lax.dot_general(
        pair_in, grad_pre, (((1,), (1,)), ((), ())), preferred_element_type=jnp.float32
    )
    grad_pair = grad_update + lax.dot_general(
        w_in, grad_pre, (((1,), (0,)), ((), ())), preferred_element_type=jnp.float32
    )
    grad_cube = grad_pair.reshape(channels, row_count, col_count)
    return (
        logits.reshape(row_count, col_count),
        head_term,
        out_term,
        in_term,
        jnp.sum(grad_pair, axis=1),
        jnp.sum(grad_cube, axis=2),
        jnp.sum(grad_cube, axis=1),
    )


def tile_terms(row_proj, col_proj, bias_col, row_flags, col_flags, goal_tile, w_in, w_out, w_head):
    half_rows = row_proj.shape[1] // 2
    first = block_terms(
        row_proj[:, :half_rows],
        col_proj,
        bias_col,
        row_flags[:half_rows],
        col_flags,
        goal_tile[:half_rows],
        w_in,
        w_out,
        w_head,
    )
    second = block_terms(
        row_proj[:, half_rows:],
        col_proj,
        bias_col,
        row_flags[half_rows:],
        col_flags,
        goal_tile[half_rows:],
        w_in,
        w_out,
        w_head,
    )
    return (
        jnp.concatenate([first[0], second[0]], axis=0),
        first[1] + second[1],
        first[2] + second[2],
        first[3] + second[3],
        first[4] + second[4],
        jnp.concatenate([first[5], second[5]], axis=1),
        first[6] + second[6],
    )


def project(embedding, weight):
    return lax.dot_general(
        weight, embedding, (((0,), (1,)), ((), ())), preferred_element_type=jnp.float32
    ).astype(jnp.bfloat16)


def fetch_ahead(right_proj, flags_low, step_count):
    return from_behind((right_proj, flags_low), "rows", -step_count)


def return_behind(col_piece, step_count):
    return from_behind(col_piece, "rows", step_count)


def on_device(
    embedding, w_left, w_right, w_in, w_out, w_head, dist_bias, offsets, valid_bins, target
):
    bin_count = embedding.shape[0]
    tile_count = bin_count // TILE
    slot_count = offsets.shape[1]
    reach_count = (NOFF + tile_count - 2) // tile_count
    channels = w_left.shape[1]
    hidden = w_in.shape[1]
    left_proj = project(embedding, w_left)
    right_proj = project(embedding, w_right)
    flags_low = valid_bins.astype(jnp.bfloat16)
    proj_parts = [right_proj]
    flag_parts = [flags_low]
    for step_count in range(1, reach_count + 1):
        moved_proj, moved_flags = fetch_ahead(right_proj, flags_low, step_count)
        proj_parts.append(moved_proj)
        flag_parts.append(moved_flags)
    right_ext = jnp.concatenate(proj_parts, axis=1)
    flags_ext = jnp.concatenate(flag_parts, axis=0).astype(jnp.float32)
    extended = bin_count * (reach_count + 1)
    initial = (
        jnp.zeros((channels, bin_count), jnp.float32),
        jnp.zeros((channels, extended), jnp.float32),
        jnp.zeros((channels, hidden), jnp.float32),
        jnp.zeros((hidden, channels), jnp.float32),
        jnp.zeros((channels,), jnp.float32),
        jnp.zeros((channels, NOFF), jnp.float32),
    )

    def advance(totals, item_index):
        tile_row = item_index // slot_count
        slot_index = item_index % slot_count
        offset = offsets[tile_row, slot_index]
        one_hot = (jnp.arange(NOFF, dtype=jnp.int32) == offset).astype(jnp.float32)
        bias_col = jnp.sum(dist_bias * one_hot[None, :], axis=1)
        row_start = tile_row * TILE
        col_start = (tile_row + offset) * TILE
        col_proj = lax.dynamic_slice_in_dim(right_ext, col_start, TILE, 1)
        row_flags = lax.dynamic_slice_in_dim(flags_ext, row_start, TILE, 0)
        col_flags = lax.dynamic_slice_in_dim(flags_ext, col_start, TILE, 0)
        goal_tile = target[tile_row, slot_index]
        logits, head_term, out_term, in_term, bias_sum, row_sums, col_sums = tile_terms(
            left_proj, col_proj, bias_col, row_flags, col_flags, goal_tile, w_in, w_out, w_head
        )
        row_acc, col_acc, in_acc, out_acc, head_acc, bias_acc = totals
        row_acc = row_acc + row_sums
        col_acc = lax.dynamic_update_slice_in_dim(
            col_acc, lax.dynamic_slice_in_dim(col_acc, col_start, TILE, 1) + col_sums, col_start, 1
        )
        bias_acc = bias_acc + bias_sum[:, None] * one_hot[None, :]
        return (
            (
                row_acc,
                col_acc,
                in_acc + in_term,
                out_acc + out_term,
                head_acc + head_term,
                bias_acc,
            ),
            logits,
        )

    totals, logits = lax.scan(
        advance, initial, jnp.arange(tile_count * slot_count, dtype=jnp.int32)
    )
    row_acc, col_acc, in_part, out_part, head_part, bias_part = totals
    predicted = logits.reshape(tile_count, slot_count, TILE, TILE).astype(jnp.bfloat16)
    col_own = col_acc[:, :bin_count]
    for step_count in range(1, reach_count + 1):
        col_piece = col_acc[:, step_count * bin_count : (step_count + 1) * bin_count]
        col_own = col_own + return_behind(col_piece, step_count)
    row_total, col_total = lax.psum((row_acc, col_own), "band")
    row_grad = row_total.astype(jnp.bfloat16)
    col_grad = col_total.astype(jnp.bfloat16)
    grad_in, grad_out, grad_head, grad_bias = lax.psum(
        (in_part, out_part, head_part, bias_part), ("rows", "band")
    )
    share = embedding.shape[1] // lax.axis_size("band")
    share_start = lax.axis_index("band") * share
    left_share = lax.dynamic_slice_in_dim(w_left, share_start, share, 0)
    right_share = lax.dynamic_slice_in_dim(w_right, share_start, share, 0)
    grad_embedding = (
        lax.dot_general(
            row_grad, left_share, (((0,), (1,)), ((), ())), preferred_element_type=jnp.float32
        )
        + lax.dot_general(
            col_grad, right_share, (((0,), (1,)), ((), ())), preferred_element_type=jnp.float32
        )
    ).astype(jnp.bfloat16)
    embed_share = lax.dynamic_slice_in_dim(embedding, share_start, share, 1)
    left_part = lax.dot_general(
        embed_share, row_grad, (((0,), (1,)), ((), ())), preferred_element_type=jnp.float32
    )
    right_part = lax.dot_general(
        embed_share, col_grad, (((0,), (1,)), ((), ())), preferred_element_type=jnp.float32
    )
    left_sum, right_sum = lax.psum((left_part, right_part), "rows")
    grad_left, grad_right = (
        lax.all_gather(left_sum, "band", axis=0, tiled=True),
        lax.all_gather(right_sum, "band", axis=0, tiled=True),
    )
    return (
        predicted,
        grad_embedding,
        grad_left,
        grad_right,
        grad_in,
        grad_out,
        grad_head,
        grad_bias,
    )


def solution(mesh):
    placed = (
        P("rows", None),
        P(),
        P(),
        P(),
        P(),
        P(),
        P(),
        P("rows", "band"),
        P("rows"),
        P("rows", "band", None, None),
    )
    return jax.shard_map(
        on_device,
        mesh=mesh,
        in_specs=placed,
        out_specs=(P("rows", "band", None, None), P("rows", "band"), P(), P(), P(), P(), P(), P()),
        check_vma=False,
    )
```

profile of v0, /device:TPU:0, one launch (start us, length us, event | category | flops | bytes accessed | tf_op | source)
XLA Modules:
  0.0 160.9 jit_solution(8311720177533387643)
XLA Ops:
  0.6 0.9 copy-done
  1.5 0.9 convolution_convert_fusion
  2.4 1.3 collective-permute-start
  3.7 1.3 collective-permute-start.1
  5.7 1.3 collective-permute-start.3
  7.0 1.3 collective-permute-start.4
  8.3 1.3 collective-permute-start.5
  10.2 0.9 convolution_convert_fusion.1
  12.8 1.3 collective-permute-start.2
  14.1 2.7 %collective-permute-done.4 = bf16[128]{0:T(256)(128)(2,1)S(1)} collective-permute-done((bf16[128]{0:T(256)(128)(2,1)S(1)}, bf16[128]{0:T(256)(128)(2,1)S(1)}, u32[]{:S(2)}, u32[]{:S(2)}) %collective-permute-start.4) | collective-permute-done | bytes 288 | tf_op jit(solution)/shard_map/ppermute | solution.py:13
  16.8 3.4 %collective-permute-done.5 = bf16[128]{0:T(256)(128)(2,1)S(1)} collective-permute-done((bf16[128]{0:T(256)(128)(2,1)S(1)}, bf16[128]{0:T(256)(128)(2,1)S(1)}, u32[]{:S(2)}, u32[]{:S(2)}) %collective-permute-start.5) | collective-permute-done | bytes 288 | tf_op jit(solution)/shard_map/ppermute | solution.py:13
  20.3 4.3 %collective-permute-done.2 = bf16[32,128]{1,0:T(8,128)(2,1)S(1)} collective-permute-done((bf16[32,128]{1,0:T(8,128)(2,1)S(1)}, bf16[32,128]{1,0:T(8,128)(2,1)S(1)}, u32[]{:S(2)}, u32[]{:S(2)}) %collective-permute-start.2) | collective-permute-done | bytes 8224 | tf_op jit(solution)/shard_map/ppermute | solution.py:13
  25.2 2.7 %multiply_convert_fusion = (bf16[128,8192]{0,1:T(8,128)(2,1)S(1)}, f32[128,8192]{0,1:T(8,128)S(1)}) fusion(bf16[32,128]{1,0:T(8,128)(2,1)} %param.13, f32[4,8,64,128]{3,2,1,0:T(8,128)S(1)} %bitcast.119, f32[32]{0:T(128)S(1)} %multiply_reduce_fusion), kind=kOutput, calls=%fused_computation.30 | convolution fusion | flops 77070336 | bytes 7348352 | tf_op jit(solution)/shard_map/while/body/eval_jaxpr/dot_general | solution.py:31
  28.0 2.0 %multiply_convert_fusion.1 = (bf16[128,8192]{0,1:T(8,128)(2,1)S(1)}, f32[128,8192]{0,1:T(8,128)S(1)}) fusion(bf16[32,128]{1,0:T(8,128)(2,1)S(1)} %copy-done.2, f32[4,8,64,128]{3,2,1,0:T(8,128)S(1)} %bitcast.122, f32[32]{0:T(128)S(1)} %multiply_reduce_fusion), kind=kOutput, calls=%fused_computation.31 | convolution fusion | flops 77070336 | bytes 7348352 | tf_op jit(solution)/shard_map/while/body/eval_jaxpr/dot_general | solution.py:31
  30.0 1.0 fusion.2
  31.0 1.0 fusion.3
  33.9 3.7 %fusion.10 = bf16[128,8192]{0,1:T(8,128)(2,1)S(1)} fusion(f32[128,8192]{0,1:T(8,128)S(1)} %get-tuple-element.81, bf16[128,32]{0,1:T(8,128)(2,1)S(1)} %copy-done.1, f32[8192]{0:T(1024)S(1)} %get-tuple-element.70, f32[32]{0:T(128)S(1)} %copy-done.4), kind=kOutput, calls=%fused_computation.22 | convolution fusion | flops 88604672 | bytes 6332544 | tf_op jit(solution)/shard_map/while/body/eval_jaxpr/dot_general | solution.py:47
  37.6 0.9 fusion.67
  39.3 3.5 %fusion.17 = bf16[128,8192]{0,1:T(8,128)(2,1)S(1)} fusion(f32[128,8192]{0,1:T(8,128)S(1)} %get-tuple-element.83, bf16[128,32]{0,1:T(8,128)(2,1)S(1)} %copy-done.1, f32[8192]{0:T(1024)S(1)} %get-tuple-element.71, f32[32]{0:T(128)S(1)} %copy-done.4), kind=kOutput, calls=%fused_computation.29 | convolution fusion | flops 88604672 | bytes 6332544 | tf_op jit(solution)/shard_map/while/body/eval_jaxpr/dot_general | solution.py:47
  42.8 0.9 fusion.68
  44.4 1.4 convolution_bitcast_fusion.8
  47.7 3.4 %collective-permute-start.6 = (f32[32,128]{1,0:T(8,128)S(1)}, f32[32,128]{1,0:T(8,128)S(1)}, u32[]{:S(2)}, u32[]{:S(2)}) collective-permute-start(f32[32,128]{1,0:T(8,128)S(1)} %get-tuple-element.50), channel_id=1, source_target_pairs={{0,4},{4,8},{8,12},{12,16},{16,20},{20,24},{24,28},{1,5},{5,9},{9,... | collective-permute-start | bytes 49160 | tf_op jit(solution)/shard_map/ppermute | solution.py:13
  51.2 4.8 %collective-permute-start.7 = (f32[32,128]{1,0:T(8,128)S(1)}, f32[32,128]{1,0:T(8,128)S(1)}, u32[]{:S(2)}, u32[]{:S(2)}) collective-permute-start(f32[32,128]{1,0:T(8,128)S(1)} %get-tuple-element.69), channel_id=1, source_target_pairs={{0,8},{4,12},{8,16},{12,20},{16,24},{20,28},{1,9},{5,13},{9,17},{1... | collective-permute-start | bytes 49160 | tf_op jit(solution)/shard_map/ppermute | solution.py:13
  55.9 2.0 %collective-permute-start.8 = (f32[32,128]{1,0:T(8,128)S(1)}, f32[32,128]{1,0:T(8,128)S(1)}, u32[]{:S(2)}, u32[]{:S(2)}) collective-permute-start(f32[32,128]{1,0:T(8,128)S(1)} %get-tuple-element.68), channel_id=1, source_target_pairs={{0,12},{4,16},{8,20},{12,24},{16,28},{1,13},{5,17},{9,21},{13,25},... | collective-permute-start | bytes 49160 | tf_op jit(solution)/shard_map/ppermute | solution.py:13
  58.6 1.6 fusion.19
  60.9 39.1 %all-reduce = (f32[32,128]{1,0:T(8,128)}, f32[128,32]{0,1:T(8,128)}, f32[32]{0:T(128)}, f32[32,4]{0,1:T(4,128)}) all-reduce(f32[32,128]{1,0:T(8,128)S(1)} %convolution_add_fusion.2, f32[128,32]{0,1:T(8,128)S(1)} %convolution_add_fusion.1, f32[32]{0:T(128)S(1)} %fusion.19, ...), channel_id=1, replica_groups=mesh['rows'=8,'band'=4] {'rows','band'}, use_global_device_ids=true, to_apply=%region_9.10 | all-reduce | flops 8352 | bytes 66816 | tf_op jit(solution)/shard_map/psum | solution.py:194
  100.1 10.3 %all-reduce.2 = (bf16[32,128]{1,0:T(8,128)(2,1)S(1)}, bf16[32,128]{1,0:T(8,128)(2,1)S(1)}) all-reduce(f32[32,128]{1,0:T(8,128)S(1)} %pad_maximum_fusion.1, f32[32,128]{1,0:T(8,128)S(1)} %fusion.40), channel_id=1, replica_groups=mesh['rows'=8,'band'=4] {'band'}, use_global_device_ids=true, to_apply=%region_3.4 | all-reduce | flops 8192 | bytes 49152 | tf_op jit(solution)/shard_map/psum | solution.py:191
  110.5 0.9 fusion.46
  111.5 36.1 %all-reduce.1 = (f32[128,32]{0,1:T(8,128)S(1)}, f32[128,32]{0,1:T(8,128)S(1)}) all-reduce(f32[128,32]{0,1:T(8,128)S(1)} %fusion.35, f32[128,32]{0,1:T(8,128)S(1)} %fusion.37), channel_id=1, replica_groups=mesh['rows'=8,'band'=4] {'rows'}, use_global_device_ids=true, to_apply=%region_7.8 | all-reduce | flops 8192 | bytes 65536 | tf_op jit(solution)/shard_map/psum | solution.py:216
  147.7 5.2 %all_gather.6 = f32[512,32]{0,1:T(8,128)S(1)} all-gather(f32[128,32]{0,1:T(8,128)S(1)} %get-tuple-element.46), channel_id=1, replica_groups=mesh['rows'=8,'band'=4] {'band'}, dimensions={0}, use_global_device_ids=true | all-gather | bytes 81920 | tf_op jit(solution)/shard_map/all_gather | solution.py:218
  152.9 5.2 %all_gather.7 = f32[512,32]{0,1:T(8,128)S(1)} all-gather(f32[128,32]{0,1:T(8,128)S(1)} %get-tuple-element.47), channel_id=1, replica_groups=mesh['rows'=8,'band'=4] {'band'}, dimensions={0}, use_global_device_ids=true | all-gather | bytes 81920 | tf_op jit(solution)/shard_map/all_gather | solution.py:219
  158.1 1.5 fusion.18
  (48 shorter events, 11.2 us)
Async XLA Ops:
  0.6 0.9 copy-start
  2.4 17.9 %collective-permute-start = (bf16[32,128]{1,0:T(8,128)(2,1)S(1)}, bf16[32,128]{1,0:T(8,128)(2,1)S(1)}, u32[]{:S(2)}, u32[]{:S(2)}) collective-permute-start(bf16[32,128]{1,0:T(8,128)(2,1)S(1)} %convolution_convert_fusion), channel_id=1, source_target_pairs={{4,0},{8,4},{12,8},{16,12},{20,16},{24,20},{28,24},{5,1},{9,5},{13... | collective-permute-start | bytes 24584 | tf_op jit(solution)/shard_map/ppermute | solution.py:13
  3.7 16.6 %collective-permute-start.1 = (bf16[32,128]{1,0:T(8,128)(2,1)S(1)}, bf16[32,128]{1,0:T(8,128)(2,1)S(1)}, u32[]{:S(2)}, u32[]{:S(2)}) collective-permute-start(bf16[32,128]{1,0:T(8,128)(2,1)S(1)} %convolution_convert_fusion), channel_id=1, source_target_pairs={{8,0},{12,4},{16,8},{20,12},{24,16},{28,20},{9,1},{13,5},{17,9},{2... | collective-permute-start | bytes 24584 | tf_op jit(solution)/shard_map/ppermute | solution.py:13
  5.7 7.1 %collective-permute-start.3 = (bf16[128]{0:T(256)(128)(2,1)S(1)}, bf16[128]{0:T(256)(128)(2,1)S(1)}, u32[]{:S(2)}, u32[]{:S(2)}) collective-permute-start(bf16[128]{0:T(256)(128)(2,1)S(1)} %convert_element_type.109), channel_id=1, source_target_pairs={{4,0},{8,4},{12,8},{16,12},{20,16},{24,20},{28,24},{5,1},{9,5},{13... | collective-permute-start | bytes 776 | tf_op jit(solution)/shard_map/ppermute | solution.py:13
  7.0 9.8 %collective-permute-start.4 = (bf16[128]{0:T(256)(128)(2,1)S(1)}, bf16[128]{0:T(256)(128)(2,1)S(1)}, u32[]{:S(2)}, u32[]{:S(2)}) collective-permute-start(bf16[128]{0:T(256)(128)(2,1)S(1)} %convert_element_type.109), channel_id=1, source_target_pairs={{8,0},{12,4},{16,8},{20,12},{24,16},{28,20},{9,1},{13,5},{17,9},{2... | collective-permute-start | bytes 776 | tf_op jit(solution)/shard_map/ppermute | solution.py:13
  8.3 11.9 %collective-permute-start.5 = (bf16[128]{0:T(256)(128)(2,1)S(1)}, bf16[128]{0:T(256)(128)(2,1)S(1)}, u32[]{:S(2)}, u32[]{:S(2)}) collective-permute-start(bf16[128]{0:T(256)(128)(2,1)S(1)} %convert_element_type.109), channel_id=1, source_target_pairs={{12,0},{16,4},{20,8},{24,12},{28,16},{13,1},{17,5},{21,9},{25,13},... | collective-permute-start | bytes 776 | tf_op jit(solution)/shard_map/ppermute | solution.py:13
  12.8 11.8 %collective-permute-start.2 = (bf16[32,128]{1,0:T(8,128)(2,1)S(1)}, bf16[32,128]{1,0:T(8,128)(2,1)S(1)}, u32[]{:S(2)}, u32[]{:S(2)}) collective-permute-start(bf16[32,128]{1,0:T(8,128)(2,1)S(1)} %convolution_convert_fusion), channel_id=1, source_target_pairs={{12,0},{16,4},{20,8},{24,12},{28,16},{13,1},{17,5},{21,9},{25,13},... | collective-permute-start | bytes 24584 | tf_op jit(solution)/shard_map/ppermute | solution.py:13
  25.2 2.8 %copy-start.2 = (bf16[32,128]{1,0:T(8,128)(2,1)S(1)}, bf16[32,128]{1,0:T(8,128)(2,1)}, u32[]{:S(2)}) copy-start(bf16[32,128]{1,0:T(8,128)(2,1)} %param.13) | copy-start | bytes 24580
  28.0 2.0 %copy-start.1 = (bf16[128,32]{0,1:T(8,128)(2,1)S(1)}, bf16[128,32]{0,1:T(8,128)(2,1)}, u32[]{:S(2)}) copy-start(bf16[128,32]{0,1:T(8,128)(2,1)} %param.14) | copy-start | bytes 24580
  30.0 2.0 %copy-start.4 = (f32[32]{0:T(128)S(1)}, f32[32]{0:T(128)}, u32[]{:S(2)}) copy-start(f32[32]{0:T(128)} %param.15) | copy-start | bytes 388
  31.0 2.3 %copy-start.3 = (bf16[1,1,128,128]{3,2,1,0:T(8,128)(2,1)S(1)}, bf16[1,1,128,128]{3,2,1,0:T(8,128)(2,1)}, u32[]{:S(2)}) copy-start(bf16[1,1,128,128]{3,2,1,0:T(8,128)(2,1)} %param.19) | copy-start | bytes 98308
  47.7 52.3 %collective-permute-start.6 = (f32[32,128]{1,0:T(8,128)S(1)}, f32[32,128]{1,0:T(8,128)S(1)}, u32[]{:S(2)}, u32[]{:S(2)}) collective-permute-start(f32[32,128]{1,0:T(8,128)S(1)} %get-tuple-element.50), channel_id=1, source_target_pairs={{0,4},{4,8},{8,12},{12,16},{16,20},{20,24},{24,28},{1,5},{5,9},{9,... | collective-permute-start | bytes 49160 | tf_op jit(solution)/shard_map/ppermute | solution.py:13
  51.2 48.9 %collective-permute-start.7 = (f32[32,128]{1,0:T(8,128)S(1)}, f32[32,128]{1,0:T(8,128)S(1)}, u32[]{:S(2)}, u32[]{:S(2)}) collective-permute-start(f32[32,128]{1,0:T(8,128)S(1)} %get-tuple-element.69), channel_id=1, source_target_pairs={{0,8},{4,12},{8,16},{12,20},{16,24},{20,28},{1,9},{5,13},{9,17},{1... | collective-permute-start | bytes 49160 | tf_op jit(solution)/shard_map/ppermute | solution.py:13
  55.9 44.1 %collective-permute-start.8 = (f32[32,128]{1,0:T(8,128)S(1)}, f32[32,128]{1,0:T(8,128)S(1)}, u32[]{:S(2)}, u32[]{:S(2)}) collective-permute-start(f32[32,128]{1,0:T(8,128)S(1)} %get-tuple-element.68), channel_id=1, source_target_pairs={{0,12},{4,16},{8,20},{12,24},{16,28},{1,13},{5,17},{9,21},{13,25},... | collective-permute-start | bytes 49160 | tf_op jit(solution)/shard_map/ppermute | solution.py:13
where the time goes:
time: 162 us; the launch traced here: 161 us
  blocking collectives  96 us (59%)
  matrix products  27 us (17%)
  starting transfers between devices  17.9 us (11%)
  waiting for transfers between devices  11.1 us (7%)
  other arithmetic  4.46 us (3%)
  local copies, waits for them, and re-layouts  2.72 us (2%)
  between operations  1.62 us (1%)
    psum x1, blocking collectives, on_device(): lax.psum((in_part, out_part, head_part, bias_part), ('rows', 'band'))  39.1 us
    psum x1, blocking collectives, on_device(): left_sum, right_sum = lax.psum((left_part, right_part), 'rows')  36.1 us
    ppermute x9, starting transfers between devices, from_behind(): lax.ppermute(value, axis, [(source, source + steps) for source in range(l...  17.9 us
    ppermute x9, waiting for transfers between devices, from_behind(): lax.ppermute(value, axis, [(source, source + steps) for source in range(l...  11.1 us
    psum x1, blocking collectives, on_device(): row_total, col_total = lax.psum((row_acc, col_own), 'band')  10.3 us
    dot_general x2, matrix products, block_terms(): lax.dot_general(w_out, grad_low, (((1,), (0,)), ((), ())), preferred_elem...  7.13 us
    all_gather x1, blocking collectives, on_device(): lax.all_gather(left_sum, 'band', axis=0, tiled=True)  5.22 us
    all_gather x1, blocking collectives, on_device(): lax.all_gather(right_sum, 'band', axis=0, tiled=True)  5.22 us
  transfers between devices with their start and end apart: 9, of which 4 were waited for; matrix products, arithmetic and copies ran while one was open for 3% of the time, Pallas kernels for 0%

commit v1 on v0

--- a/solution.py
+++ b/solution.py
@@ -119,6 +119,11 @@
 def on_device(
     embedding, w_left, w_right, w_in, w_out, w_head, dist_bias, offsets, valid_bins, target
 ):
+
+    def update_teams(local, mesh_dim, along_axis):
+        block_out = lax.psum(local, mesh_dim)
+        return lax.psum(block_out, along_axis)
+
     bin_count = embedding.shape[0]
     tile_count = bin_count // TILE
     slot_count = offsets.shape[1]
@@ -191,8 +196,8 @@
     row_total, col_total = lax.psum((row_acc, col_own), "band")
     row_grad = row_total.astype(jnp.bfloat16)
     col_grad = col_total.astype(jnp.bfloat16)
-    grad_in, grad_out, grad_head, grad_bias = lax.psum(
-        (in_part, out_part, head_part, bias_part), ("rows", "band")
+    grad_in, grad_out, grad_head, grad_bias = update_teams(
+        (in_part, out_part, head_part, bias_part), "band", "rows"
     )
     share = embedding.shape[1] // lax.axis_size("band")
     share_start = lax.axis_index("band") * share

time: 162 us -> 176 us (1.086)
  blocking collectives: 96 us -> 22.9 us
  waiting for transfers between devices: 11.1 us -> 79.1 us
  between operations: 1.62 us -> 15 us
  local copies, waits for them, and re-layouts: 2.72 us -> 7.75 us
    psum x2 -> x0, blocking collectives: 75.2 us -> none  [the longest x1 39.1 us: on_device(): lax.psum((in_part, out_part, head_part, bias_part), ('rows', 'band'))]
    psum x0 -> x1, waiting for transfers between devices: none -> 68 us  [on_device(): left_sum, right_sum = lax.psum((left_part, right_part), 'rows')]
    unnamed x14 -> x18, local copies, waits for them, and re-layouts: 2.56 us -> 7.59 us
  transfers between devices with their start and end apart: 9 -> 10, of which waited for: 4 -> 5; matrix products, arithmetic and copies ran while one was open for 3% -> 4% of each run, Pallas kernels for 0% -> 0%
where the time goes in v1:
time: 176 us; the launch traced here: 175 us
  waiting for transfers between devices  79.1 us (45%)
  matrix products  28.3 us (16%)
  blocking collectives  22.9 us (13%)
  starting transfers between devices  17.9 us (10%)
  between operations  15 us (9%)
  local copies, waits for them, and re-layouts  7.75 us (4%)
  other arithmetic  4.46 us (3%)
    psum x1, waiting for transfers between devices, on_device(): left_sum, right_sum = lax.psum((left_part, right_part), 'rows')  68 us
    ppermute x9, starting transfers between devices, from_behind(): lax.ppermute(value, axis, [(source, source + steps) for source in range(l...  17.9 us
    psum x1, blocking collectives, on_device(): row_total, col_total = lax.psum((row_acc, col_own), 'band')  12 us
    ppermute x9, waiting for transfers between devices, from_behind(): lax.ppermute(value, axis, [(source, source + steps) for source in range(l...  11.1 us
    unnamed x18, local copies, waits for them, and re-layouts  7.59 us
    dot_general x2, matrix products, block_terms(): lax.dot_general(w_out, grad_low, (((1,), (0,)), ((), ())), preferred_elem...  7.12 us
    all_gather x1, blocking collectives, on_device(): lax.all_gather(right_sum, 'band', axis=0, tiled=True)  5.43 us
    all_gather x1, blocking collectives, on_device(): lax.all_gather(left_sum, 'band', axis=0, tiled=True)  5.43 us
  transfers between devices with their start and end apart: 10, of which 5 were waited for; matrix products, arithmetic and copies ran while one was open for 4% of the time, Pallas kernels for 0%

profile of v1, /device:TPU:0, one launch (start us, length us, event | category | flops | bytes accessed | tf_op | source)
XLA Modules:
  0.0 175.4 jit_solution(346986660405215727)
XLA Ops:
  9.0 1.3 collective-permute-start
  10.3 1.3 collective-permute-start.1
  12.2 1.3 collective-permute-start.3
  13.5 1.3 collective-permute-start.4
  14.8 1.3 collective-permute-start.5
  16.8 0.9 convolution_convert_fusion.1
  19.3 1.3 collective-permute-start.2
  20.6 2.7 %collective-permute-done.4 = bf16[128]{0:T(256)(128)(2,1)S(1)} collective-permute-done((bf16[128]{0:T(256)(128)(2,1)S(1)}, bf16[128]{0:T(256)(128)(2,1)S(1)}, u32[]{:S(2)}, u32[]{:S(2)}) %collective-permute-start.4) | collective-permute-done | bytes 288 | tf_op jit(solution)/shard_map/ppermute | solution.py:13
  23.3 3.4 %collective-permute-done.5 = bf16[128]{0:T(256)(128)(2,1)S(1)} collective-permute-done((bf16[128]{0:T(256)(128)(2,1)S(1)}, bf16[128]{0:T(256)(128)(2,1)S(1)}, u32[]{:S(2)}, u32[]{:S(2)}) %collective-permute-start.5) | collective-permute-done | bytes 288 | tf_op jit(solution)/shard_map/ppermute | solution.py:13
  26.9 4.3 %collective-permute-done.2 = bf16[32,128]{1,0:T(8,128)(2,1)S(1)} collective-permute-done((bf16[32,128]{1,0:T(8,128)(2,1)S(1)}, bf16[32,128]{1,0:T(8,128)(2,1)S(1)}, u32[]{:S(2)}, u32[]{:S(2)}) %collective-permute-start.2) | collective-permute-done | bytes 8224 | tf_op jit(solution)/shard_map/ppermute | solution.py:13
  31.8 2.7 %multiply_convert_fusion = (bf16[128,8192]{0,1:T(8,128)(2,1)S(1)}, f32[128,8192]{0,1:T(8,128)S(1)}) fusion(bf16[32,128]{1,0:T(8,128)(2,1)} %param.13, f32[4,8,64,128]{3,2,1,0:T(8,128)S(1)} %bitcast.119, f32[32]{0:T(128)S(1)} %multiply_reduce_fusion), kind=kOutput, calls=%fused_computation.30 | convolution fusion | flops 77070336 | bytes 7348352 | tf_op jit(solution)/shard_map/while/body/eval_jaxpr/dot_general | solution.py:31
  34.5 2.0 %multiply_convert_fusion.1 = (bf16[128,8192]{0,1:T(8,128)(2,1)S(1)}, f32[128,8192]{0,1:T(8,128)S(1)}) fusion(bf16[32,128]{1,0:T(8,128)(2,1)S(1)} %copy-done.2, f32[4,8,64,128]{3,2,1,0:T(8,128)S(1)} %bitcast.122, f32[32]{0:T(128)S(1)} %multiply_reduce_fusion), kind=kOutput, calls=%fused_computation.31 | convolution fusion | flops 77070336 | bytes 7348352 | tf_op jit(solution)/shard_map/while/body/eval_jaxpr/dot_general | solution.py:31
  36.5 1.0 fusion.2
  37.5 1.0 fusion.3
  40.4 3.7 %fusion.10 = bf16[128,8192]{0,1:T(8,128)(2,1)S(1)} fusion(f32[128,8192]{0,1:T(8,128)S(1)} %get-tuple-element.85, bf16[128,32]{0,1:T(8,128)(2,1)S(1)} %copy-done.1, f32[8192]{0:T(1024)S(1)} %get-tuple-element.74, f32[32]{0:T(128)S(1)} %copy-done.4), kind=kOutput, calls=%fused_computation.22 | convolution fusion | flops 88604672 | bytes 6332544 | tf_op jit(solution)/shard_map/while/body/eval_jaxpr/dot_general | solution.py:47
  44.1 0.9 fusion.67
  45.9 3.5 %fusion.17 = bf16[128,8192]{0,1:T(8,128)(2,1)S(1)} fusion(f32[128,8192]{0,1:T(8,128)S(1)} %get-tuple-element.87, bf16[128,32]{0,1:T(8,128)(2,1)S(1)} %copy-done.1, f32[8192]{0:T(1024)S(1)} %get-tuple-element.75, f32[32]{0:T(128)S(1)} %copy-done.4), kind=kOutput, calls=%fused_computation.29 | convolution fusion | flops 88604672 | bytes 6332544 | tf_op jit(solution)/shard_map/while/body/eval_jaxpr/dot_general | solution.py:47
  49.3 0.9 fusion.68
  50.9 1.4 convolution_bitcast_fusion.8
  54.3 3.4 %collective-permute-start.6 = (f32[32,128]{1,0:T(8,128)S(1)}, f32[32,128]{1,0:T(8,128)S(1)}, u32[]{:S(2)}, u32[]{:S(2)}) collective-permute-start(f32[32,128]{1,0:T(8,128)S(1)} %get-tuple-element.71), channel_id=1, source_target_pairs={{0,4},{4,8},{8,12},{12,16},{16,20},{20,24},{24,28},{1,5},{5,9},{9,... | collective-permute-start | bytes 49160 | tf_op jit(solution)/shard_map/ppermute | solution.py:13
  57.7 4.8 %collective-permute-start.7 = (f32[32,128]{1,0:T(8,128)S(1)}, f32[32,128]{1,0:T(8,128)S(1)}, u32[]{:S(2)}, u32[]{:S(2)}) collective-permute-start(f32[32,128]{1,0:T(8,128)S(1)} %get-tuple-element.73), channel_id=1, source_target_pairs={{0,8},{4,12},{8,16},{12,20},{16,24},{20,28},{1,9},{5,13},{9,17},{1... | collective-permute-start | bytes 49160 | tf_op jit(solution)/shard_map/ppermute | solution.py:13
  62.5 2.0 %collective-permute-start.8 = (f32[32,128]{1,0:T(8,128)S(1)}, f32[32,128]{1,0:T(8,128)S(1)}, u32[]{:S(2)}, u32[]{:S(2)}) collective-permute-start(f32[32,128]{1,0:T(8,128)S(1)} %get-tuple-element.72), channel_id=1, source_target_pairs={{0,12},{4,16},{8,20},{12,24},{16,28},{1,13},{5,17},{9,21},{13,25},... | collective-permute-start | bytes 49160 | tf_op jit(solution)/shard_map/ppermute | solution.py:13
  65.1 1.6 fusion.19
  67.5 12.0 %all-reduce.1 = (bf16[32,128]{1,0:T(8,128)(2,1)S(1)}, bf16[32,128]{1,0:T(8,128)(2,1)S(1)}, f32[32,128]{1,0:T(8,128)}, f32[128,32]{0,1:T(8,128)}, f32[32]{0:T(128)}, /*index=5*/f32[32,4]{0,1:T(4,128)}) all-reduce(f32[32,128]{1,0:T(8,128)S(1)} %pad_maximum_fusion.1, ...), channel_id=1, replica_groups=mesh['rows'=8,'band'=4] {'band'}, use_global_device_ids=true, to_apply=%region_3.4 | all-reduce | flops 16544 | bytes 115968 | tf_op jit(solution)/shard_map/psum | solution.py:196
  81.9 1.5 fusion.18
  83.4 68.0 %all-reduce.4.cloned.1.call-done = (f32[128,32]{0,1:T(8,128)}, f32[128,32]{0,1:T(8,128)}, f32[32,128]{1,0:T(8,128)}, f32[128,32]{0,1:T(8,128)}, f32[32]{0:T(128)}, /*index=5*/f32[32,4]{0,1:T(4,128)}) async-done(((f32[128,32]{0,1:T(8,128)}, f32[128,32]{0,1:T(8,128)}, f32[32,128]{1,0:T(8,128)}, f32[128,32]{0,1:T(8,128)}, f32[32]{0:T(128)}, /*index=5*/f32[32,4]{0,1:T(4,128)}), (f32[128,32]{0,1:T(8,128)}, ...) | async-done | bytes 66192 | tf_op jit(solution)/shard_map/psum | solution.py:221
  151.3 5.4 %all_gather.6 = f32[512,32]{0,1:T(8,128)S(1)} all-gather(f32[128,32]{0,1:T(8,128)} %get-tuple-element.42), channel_id=1, replica_groups=mesh['rows'=8,'band'=4] {'band'}, dimensions={0}, use_global_device_ids=true | all-gather | bytes 81920 | tf_op jit(solution)/shard_map/all_gather | solution.py:223
  156.8 5.4 %all_gather.7 = f32[512,32]{0,1:T(8,128)S(1)} all-gather(f32[128,32]{0,1:T(8,128)} %get-tuple-element.43), channel_id=1, replica_groups=mesh['rows'=8,'band'=4] {'band'}, dimensions={0}, use_global_device_ids=true | all-gather | bytes 81920 | tf_op jit(solution)/shard_map/all_gather | solution.py:224
  163.5 1.3 copy.52
  164.8 1.3 copy.53
  166.1 1.2 copy.54
  167.3 1.2 copy.55
  (53 shorter events, 15.1 us)
Async XLA Ops:
  7.2 0.9 copy-start
  7.2 144.2 %all-reduce.4.cloned.1.call-start = ((), (), s32[]{:S(2)}) async-start(), calls=%async_computation | async-start | bytes 136192 | tf_op jit(solution)/shard_map/psum | solution.py:221
  9.0 17.9 %collective-permute-start = (bf16[32,128]{1,0:T(8,128)(2,1)S(1)}, bf16[32,128]{1,0:T(8,128)(2,1)S(1)}, u32[]{:S(2)}, u32[]{:S(2)}) collective-permute-start(bf16[32,128]{1,0:T(8,128)(2,1)S(1)} %convolution_convert_fusion), channel_id=1, source_target_pairs={{4,0},{8,4},{12,8},{16,12},{20,16},{24,20},{28,24},{5,1},{9,5},{13... | collective-permute-start | bytes 24584 | tf_op jit(solution)/shard_map/ppermute | solution.py:13
  10.3 16.6 %collective-permute-start.1 = (bf16[32,128]{1,0:T(8,128)(2,1)S(1)}, bf16[32,128]{1,0:T(8,128)(2,1)S(1)}, u32[]{:S(2)}, u32[]{:S(2)}) collective-permute-start(bf16[32,128]{1,0:T(8,128)(2,1)S(1)} %convolution_convert_fusion), channel_id=1, source_target_pairs={{8,0},{12,4},{16,8},{20,12},{24,16},{28,20},{9,1},{13,5},{17,9},{2... | collective-permute-start | bytes 24584 | tf_op jit(solution)/shard_map/ppermute | solution.py:13
  12.2 7.1 %collective-permute-start.3 = (bf16[128]{0:T(256)(128)(2,1)S(1)}, bf16[128]{0:T(256)(128)(2,1)S(1)}, u32[]{:S(2)}, u32[]{:S(2)}) collective-permute-start(bf16[128]{0:T(256)(128)(2,1)S(1)} %convert_element_type.109), channel_id=1, source_target_pairs={{4,0},{8,4},{12,8},{16,12},{20,16},{24,20},{28,24},{5,1},{9,5},{13... | collective-permute-start | bytes 776 | tf_op jit(solution)/shard_map/ppermute | solution.py:13
  13.5 9.8 %collective-permute-start.4 = (bf16[128]{0:T(256)(128)(2,1)S(1)}, bf16[128]{0:T(256)(128)(2,1)S(1)}, u32[]{:S(2)}, u32[]{:S(2)}) collective-permute-start(bf16[128]{0:T(256)(128)(2,1)S(1)} %convert_element_type.109), channel_id=1, source_target_pairs={{8,0},{12,4},{16,8},{20,12},{24,16},{28,20},{9,1},{13,5},{17,9},{2... | collective-permute-start | bytes 776 | tf_op jit(solution)/shard_map/ppermute | solution.py:13
  14.8 11.9 %collective-permute-start.5 = (bf16[128]{0:T(256)(128)(2,1)S(1)}, bf16[128]{0:T(256)(128)(2,1)S(1)}, u32[]{:S(2)}, u32[]{:S(2)}) collective-permute-start(bf16[128]{0:T(256)(128)(2,1)S(1)} %convert_element_type.109), channel_id=1, source_target_pairs={{12,0},{16,4},{20,8},{24,12},{28,16},{13,1},{17,5},{21,9},{25,13},... | collective-permute-start | bytes 776 | tf_op jit(solution)/shard_map/ppermute | solution.py:13
  19.3 11.8 %collective-permute-start.2 = (bf16[32,128]{1,0:T(8,128)(2,1)S(1)}, bf16[32,128]{1,0:T(8,128)(2,1)S(1)}, u32[]{:S(2)}, u32[]{:S(2)}) collective-permute-start(bf16[32,128]{1,0:T(8,128)(2,1)S(1)} %convolution_convert_fusion), channel_id=1, source_target_pairs={{12,0},{16,4},{20,8},{24,12},{28,16},{13,1},{17,5},{21,9},{25,13},... | collective-permute-start | bytes 24584 | tf_op jit(solution)/shard_map/ppermute | solution.py:13
  31.7 2.8 %copy-start.2 = (bf16[32,128]{1,0:T(8,128)(2,1)S(1)}, bf16[32,128]{1,0:T(8,128)(2,1)}, u32[]{:S(2)}) copy-start(bf16[32,128]{1,0:T(8,128)(2,1)} %param.13) | copy-start | bytes 24580
  34.5 2.0 %copy-start.1 = (bf16[128,32]{0,1:T(8,128)(2,1)S(1)}, bf16[128,32]{0,1:T(8,128)(2,1)}, u32[]{:S(2)}) copy-start(bf16[128,32]{0,1:T(8,128)(2,1)} %param.14) | copy-start | bytes 24580
  36.5 2.0 %copy-start.4 = (f32[32]{0:T(128)S(1)}, f32[32]{0:T(128)}, u32[]{:S(2)}) copy-start(f32[32]{0:T(128)} %param.15) | copy-start | bytes 388
  37.5 2.3 %copy-start.3 = (bf16[1,1,128,128]{3,2,1,0:T(8,128)(2,1)S(1)}, bf16[1,1,128,128]{3,2,1,0:T(8,128)(2,1)}, u32[]{:S(2)}) copy-start(bf16[1,1,128,128]{3,2,1,0:T(8,128)(2,1)} %param.19) | copy-start | bytes 98308
  54.3 13.2 %collective-permute-start.6 = (f32[32,128]{1,0:T(8,128)S(1)}, f32[32,128]{1,0:T(8,128)S(1)}, u32[]{:S(2)}, u32[]{:S(2)}) collective-permute-start(f32[32,128]{1,0:T(8,128)S(1)} %get-tuple-element.71), channel_id=1, source_target_pairs={{0,4},{4,8},{8,12},{12,16},{16,20},{20,24},{24,28},{1,5},{5,9},{9,... | collective-permute-start | bytes 49160 | tf_op jit(solution)/shard_map/ppermute | solution.py:13
  57.7 9.8 %collective-permute-start.7 = (f32[32,128]{1,0:T(8,128)S(1)}, f32[32,128]{1,0:T(8,128)S(1)}, u32[]{:S(2)}, u32[]{:S(2)}) collective-permute-start(f32[32,128]{1,0:T(8,128)S(1)} %get-tuple-element.73), channel_id=1, source_target_pairs={{0,8},{4,12},{8,16},{12,20},{16,24},{20,28},{1,9},{5,13},{9,17},{1... | collective-permute-start | bytes 49160 | tf_op jit(solution)/shard_map/ppermute | solution.py:13
  62.5 5.0 %collective-permute-start.8 = (f32[32,128]{1,0:T(8,128)S(1)}, f32[32,128]{1,0:T(8,128)S(1)}, u32[]{:S(2)}, u32[]{:S(2)}) collective-permute-start(f32[32,128]{1,0:T(8,128)S(1)} %get-tuple-element.72), channel_id=1, source_target_pairs={{0,12},{4,16},{8,20},{12,24},{16,28},{1,13},{5,17},{9,21},{13,25},... | collective-permute-start | bytes 49160 | tf_op jit(solution)/shard_map/ppermute | solution.py:13
Sparse Core Ops, SparseCore 0:
  82.0 69.3 all-reduce.3
